TPU v7x, 256 devices: a whole 4x4x8 slice. The times are simulated.
256 devices in a mesh: chan: 8 (over x, core), ctx: 32 (over z, y).
Axes of the slice: x: 4, y: 4, z: 8, core: 2. Of those that a mesh axis runs over, the one named last changes fastest.
Arguments:
- queries: bfloat16 [4096, 8192], P('ctx', 'chan'), may hold values from -6 to 6
- keys: bfloat16 [4096, 8192], P('ctx', 'chan'), may hold values from -6 to 6
- values: bfloat16 [4096, 8192], P('ctx', 'chan'), may hold values from -6 to 6
- filters: bfloat16 [4, 4096], P(None, 'ctx'), may hold values from -0.09375 to 0.09375
- cotangent: bfloat16 [4096, 8192], P('ctx', 'chan'), may hold values from -6 to 6
Outputs:
- output: bfloat16 [4096, 8192], P('ctx', 'chan')
- query_grad: bfloat16 [4096, 8192], P('ctx', 'chan')
- key_grad: bfloat16 [4096, 8192], P('ctx', 'chan')
- value_grad: bfloat16 [4096, 8192], P('ctx', 'chan')
- filter_grad: float32 [4, 4096], P(None, 'ctx')
All inputs are finite; a program needn't handle non-finite values.
Results may differ from a plain program's by a relative error of at most 0.015.
Values may be sent and summed in bfloat16 or wider, within the bound.
A program may use at most 64 MiB of HBM per device.

v0:
```python
import jax
import jax.numpy as jnp
from jax import lax
from jax.sharding import PartitionSpec as P

D = 8192
NFILT = 4


def toeplitz(padded, base, height, breadth):
    middle = padded.shape[1] // 2
    span = height + breadth - 1
    window = lax.dynamic_slice_in_dim(padded, middle + base - breadth + 1, span, 1)
    flipped = window[:, ::-1]
    tiled = jnp.tile(flipped, (1, height + 1))
    flat = tiled[:, height - 1 : height - 1 + height * (span - 1)]
    return flat.reshape(padded.shape[0], height, span - 1)[:, :, :breadth]


def diagonal_sums(product):
    nfil, height, breadth = product.shape
    stride = height + breadth
    flipped = product[:, :, ::-1]
    padded = jnp.pad(flipped, ((0, 0), (0, 0), (0, height)))
    flat = padded.reshape(nfil, height * stride)[:, : height * (stride - 1)]
    return jnp.sum(flat.reshape(nfil, height, stride - 1), axis=1)


def add_lags(lag_acc, sums, first_lag):
    middle = lag_acc.shape[1] // 2
    where = middle + first_lag
    current = lax.dynamic_slice_in_dim(lag_acc, where, sums.shape[1], 1)
    return lax.dynamic_update_slice_in_dim(lag_acc, current + sums, where, 1)


def in_blocks(block_fn, carry, piece, rows):
    count = piece.shape[0]
    size = rows * max(1, 512 // rows)
    parts = piece.reshape((count // size, size) + piece.shape[1:])
    offsets = jnp.arange(count // size, dtype=jnp.int32) * size

    def visit(state, item):
        block, offset = item
        return (block_fn(state, block, offset), None)

    result, unused = lax.scan(visit, carry, (parts, offsets))
    return result


def shards(queries, keys, values, filters, cotangent):
    rows, width = queries.shape
    nfil = filters.shape[0]
    narrow = width // nfil
    gated = (keys.astype(jnp.float32) * values.astype(jnp.float32)).astype(jnp.bfloat16)
    back = (cotangent.astype(jnp.float32) * queries.astype(jnp.float32)).astype(jnp.bfloat16)
    taps = lax.all_gather(filters, "ctx", axis=1, tiled=True)
    total = taps.shape[1]
    padded = jnp.concatenate([jnp.zeros_like(taps), taps], axis=1)
    lag_start = jnp.zeros((nfil, 2 * total), jnp.float32)
    first = lax.axis_index("ctx") * rows
    back_cols = back.reshape(rows, narrow, nfil)

    def forward_block(carry, piece, start):
        count = piece.shape[0]

        def forward_work(state):
            mixed_acc, lag_acc = state
            tile = toeplitz(padded, first - start, rows, count)
            columns = piece.reshape(count, narrow, nfil)
            mixed_acc = mixed_acc + jnp.einsum(
                "fst,tcf->scf", tile, columns, preferred_element_type=jnp.float32
            )
            product = jnp.einsum(
                "scf,tcf->fst", back_cols, columns, preferred_element_type=jnp.float32
            )
            lag_acc = add_lags(lag_acc, diagonal_sums(product), first - start - count + 1)
            return (mixed_acc, lag_acc)

        return lax.cond(start < first + rows, forward_work, lambda state: state, carry)

    empty = jnp.zeros((rows, narrow, nfil), jnp.float32)
    mixed_acc, lag_part = in_blocks(
        forward_block, (empty, lag_start), lax.all_gather(gated, "ctx", axis=0, tiled=True), rows
    )

    def backward_block(grad_acc, piece, start):
        count = piece.shape[0]

        def backward_work(state):
            tile = toeplitz(padded, start - first, count, rows)
            columns = piece.reshape(count, narrow, nfil)
            return state + jnp.einsum(
                "fst,scf->tcf", tile, columns, preferred_element_type=jnp.float32
            )

        return lax.cond(start + count > first, backward_work, lambda state: state, grad_acc)

    grad_acc = in_blocks(
        backward_block, empty, lax.all_gather(back, "ctx", axis=0, tiled=True), rows
    )
    mixed = mixed_acc.reshape(rows, width)
    gated_grad = grad_acc.reshape(rows, width)
    lag_share = lax.psum_scatter(
        lag_part[:, total:].astype(jnp.bfloat16), "ctx", scatter_dimension=1, tiled=True
    ).astype(jnp.float32)
    lag_total = lax.psum(lag_share, "chan")
    scale = (total * (D // NFILT)) ** (-0.5)
    filter_grad = lag_total * scale
    output = (queries.astype(jnp.float32) * mixed).astype(jnp.bfloat16)
    query_grad = (cotangent.astype(jnp.float32) * mixed).astype(jnp.bfloat16)
    key_grad = (gated_grad * values.astype(jnp.float32)).astype(jnp.bfloat16)
    value_grad = (gated_grad * keys.astype(jnp.float32)).astype(jnp.bfloat16)
    return (output, query_grad, key_grad, value_grad, filter_grad)


def solution(mesh):
    placed = (
        P("ctx", "chan"),
        P("ctx", "chan"),
        P("ctx", "chan"),
        P(None, "ctx"),
        P("ctx", "chan"),
    )
    return jax.shard_map(
        shards,
        mesh=mesh,
        in_specs=placed,
        out_specs=(
            P("ctx", "chan"),
            P("ctx", "chan"),
            P("ctx", "chan"),
            P("ctx", "chan"),
            P(None, "ctx"),
        ),
        check_vma=False,
    )
```

profile of v0, /device:TPU:1, one launch (start us, length us, event | category | flops | bytes accessed | tf_op | source)
XLA Modules:
  0.0 846.8 jit_solution(6806432111096197766)
XLA Ops:
  12.5 38.3 %all_gather.9 = bf16[4,4096]{1,0:T(4,128)(2,1)S(1)} all-gather(bf16[4,128]{1,0:T(4,128)(2,1)S(1)} %copy-done.7), channel_id=1, replica_groups=mesh['chan'=8,'ctx'=32] {'ctx'}, dimensions={1}, use_global_device_ids=true | all-gather | bytes 33792 | tf_op jit(solution)/shard_map/all_gather | solution.py:56
  50.8 65.4 %all-gather.5.cloned.1.call-done = bf16[4096,1024]{0,1:T(8,128)(2,1)} async-done(((bf16[128,1024]{0,1:T(8,128)(2,1)}), bf16[4096,1024]{0,1:T(8,128)(2,1)}) %all-gather.5.cloned.1.call-update) | async-done | bytes 8388624 | tf_op jit(solution)/shard_map/all_gather | solution.py:99
  116.2 7.4 copy.60
  123.7 238.9 %while.27 = (s32[]{:T(128)}, f32[128,256,4]{1,0,2:T(8,128)S(1)}, s32[8]{0:T(128)S(1)}, s32[]{:T(128)}, bf16[4,8192]{1,0:T(4,128)(2,1)S(1)}, /*index=5*/bf16[8,512,1024]{1,2,0:T(8,128)(2,1)}, s32[]{:T(128)}, s32[]{:T(128)}) while((s32[]{:T(128)}, f32[128,256,4]{1,0,2:T(8,128)S(1)}, s32[8]{0:T(128)S(1)}, s32[]{:T(128)}, ...), condition=%wide.region_8.9_spmd, body=%wide.region_5.8_spmd.sunk | while | flops 134348800 | bytes 35643552 | solution.py:46
  125.0 28.5 %conditional.5 = (f32[128,256,4]{1,0,2:T(8,128)S(1)}) conditional(s32[]{:T(128)} %convert_element_type.91, f32[128,256,4]{1,0,2:T(8,128)S(1)} %get-tuple-element.399, (s32[]{:T(128)}, s32[]{:T(128)}, bf16[4,8192]{1,0:T(4,128)(2,1)S(1)}, bf16[8,512,1024]{1,2,0:T(8,128)(2,1)}, s32[]{:T(128)}, /*index=5*/f32[128,256,4]{1,0,2:T(8,128)S(1)}) %tuple.73), branch_computations={%region_6.6_spmd, %region_7.7_spmd} | conditional | flops 134348800 | bytes 35643384 | solution.py:96
  143.5 6.8 reshape.54
  154.9 28.5 %conditional.5 = (f32[128,256,4]{1,0,2:T(8,128)S(1)}) conditional(s32[]{:T(128)} %convert_element_type.91, f32[128,256,4]{1,0,2:T(8,128)S(1)} %get-tuple-element.399, (s32[]{:T(128)}, s32[]{:T(128)}, bf16[4,8192]{1,0:T(4,128)(2,1)S(1)}, bf16[8,512,1024]{1,2,0:T(8,128)(2,1)}, s32[]{:T(128)}, /*index=5*/f32[128,256,4]{1,0,2:T(8,128)S(1)}) %tuple.73), branch_computations={%region_6.6_spmd, %region_7.7_spmd} | conditional | flops 134348800 | bytes 35643384 | solution.py:96
  173.4 6.8 reshape.54
  184.8 28.5 %conditional.5 = (f32[128,256,4]{1,0,2:T(8,128)S(1)}) conditional(s32[]{:T(128)} %convert_element_type.91, f32[128,256,4]{1,0,2:T(8,128)S(1)} %get-tuple-element.399, (s32[]{:T(128)}, s32[]{:T(128)}, bf16[4,8192]{1,0:T(4,128)(2,1)S(1)}, bf16[8,512,1024]{1,2,0:T(8,128)(2,1)}, s32[]{:T(128)}, /*index=5*/f32[128,256,4]{1,0,2:T(8,128)S(1)}) %tuple.73), branch_computations={%region_6.6_spmd, %region_7.7_spmd} | conditional | flops 134348800 | bytes 35643384 | solution.py:96
  203.2 6.8 reshape.54
  214.6 28.5 %conditional.5 = (f32[128,256,4]{1,0,2:T(8,128)S(1)}) conditional(s32[]{:T(128)} %convert_element_type.91, f32[128,256,4]{1,0,2:T(8,128)S(1)} %get-tuple-element.399, (s32[]{:T(128)}, s32[]{:T(128)}, bf16[4,8192]{1,0:T(4,128)(2,1)S(1)}, bf16[8,512,1024]{1,2,0:T(8,128)(2,1)}, s32[]{:T(128)}, /*index=5*/f32[128,256,4]{1,0,2:T(8,128)S(1)}) %tuple.73), branch_computations={%region_6.6_spmd, %region_7.7_spmd} | conditional | flops 134348800 | bytes 35643384 | solution.py:96
  233.1 6.8 reshape.54
  244.5 28.5 %conditional.5 = (f32[128,256,4]{1,0,2:T(8,128)S(1)}) conditional(s32[]{:T(128)} %convert_element_type.91, f32[128,256,4]{1,0,2:T(8,128)S(1)} %get-tuple-element.399, (s32[]{:T(128)}, s32[]{:T(128)}, bf16[4,8192]{1,0:T(4,128)(2,1)S(1)}, bf16[8,512,1024]{1,2,0:T(8,128)(2,1)}, s32[]{:T(128)}, /*index=5*/f32[128,256,4]{1,0,2:T(8,128)S(1)}) %tuple.73), branch_computations={%region_6.6_spmd, %region_7.7_spmd} | conditional | flops 134348800 | bytes 35643384 | solution.py:96
  263.0 6.8 reshape.54
  274.4 28.5 %conditional.5 = (f32[128,256,4]{1,0,2:T(8,128)S(1)}) conditional(s32[]{:T(128)} %convert_element_type.91, f32[128,256,4]{1,0,2:T(8,128)S(1)} %get-tuple-element.399, (s32[]{:T(128)}, s32[]{:T(128)}, bf16[4,8192]{1,0:T(4,128)(2,1)S(1)}, bf16[8,512,1024]{1,2,0:T(8,128)(2,1)}, s32[]{:T(128)}, /*index=5*/f32[128,256,4]{1,0,2:T(8,128)S(1)}) %tuple.73), branch_computations={%region_6.6_spmd, %region_7.7_spmd} | conditional | flops 134348800 | bytes 35643384 | solution.py:96
  292.8 6.8 reshape.54
  304.2 28.5 %conditional.5 = (f32[128,256,4]{1,0,2:T(8,128)S(1)}) conditional(s32[]{:T(128)} %convert_element_type.91, f32[128,256,4]{1,0,2:T(8,128)S(1)} %get-tuple-element.399, (s32[]{:T(128)}, s32[]{:T(128)}, bf16[4,8192]{1,0:T(4,128)(2,1)S(1)}, bf16[8,512,1024]{1,2,0:T(8,128)(2,1)}, s32[]{:T(128)}, /*index=5*/f32[128,256,4]{1,0,2:T(8,128)S(1)}) %tuple.73), branch_computations={%region_6.6_spmd, %region_7.7_spmd} | conditional | flops 134348800 | bytes 35643384 | solution.py:96
  334.1 28.5 %conditional.5 = (f32[128,256,4]{1,0,2:T(8,128)S(1)}) conditional(s32[]{:T(128)} %convert_element_type.91, f32[128,256,4]{1,0,2:T(8,128)S(1)} %get-tuple-element.399, (s32[]{:T(128)}, s32[]{:T(128)}, bf16[4,8192]{1,0:T(4,128)(2,1)S(1)}, bf16[8,512,1024]{1,2,0:T(8,128)(2,1)}, s32[]{:T(128)}, /*index=5*/f32[128,256,4]{1,0,2:T(8,128)S(1)}) %tuple.73), branch_computations={%region_6.6_spmd, %region_7.7_spmd} | conditional | flops 134348800 | bytes 35643384 | solution.py:96
  366.8 96.9 %all-gather.3.cloned.1.call-done = bf16[4096,1024]{0,1:T(8,128)(2,1)} async-done(((bf16[128,1024]{0,1:T(8,128)(2,1)}), bf16[4096,1024]{0,1:T(8,128)(2,1)}) %all-gather.3.cloned.1.call-update) | async-done | bytes 8388624 | tf_op jit(solution)/shard_map/all_gather | solution.py:83
  463.7 7.4 copy.61
  471.9 26.2 %while.26 = (s32[]{:T(128)}, f32[128,256,4]{1,0,2:T(8,128)}, f32[4,8192]{1,0:T(4,128)S(1)}, s32[8]{0:T(128)S(1)}, s32[]{:T(128)}, /*index=5*/s32[]{:T(128)}, bf1...) while((s32[]{:T(128)}, f32[128,256,4]{1,0,2:T(8,128)}, ...), condition=%wide.region_4.5_spmd, body=%wide.region_0.4_spmd.sunk | while | flops 268893696 | bytes 31679636 | solution.py:46
  473.2 16.0 %conditional.4 = ((f32[128,256,4]{1,0,2:T(8,128)}, f32[4,8192]{1,0:T(4,128)S(1)})) conditional(s32[]{:T(128)} %convert_element_type.90, (f32[128,256,4]{1,0,2:T(8,128)}, f32[4,8192]{1,0:T(4,128)S(1)}) %tuple.70, (s32[]{:T(128)}, s32[]{:T(128)}, bf16[4,8192]{1,0:T(4,128)(2,1)}, bf16[8,512,1024]{1,2,0:T(8,128)(2,1)}, s32[]{:T(128)}, ...), branch_computations={%region_1.1_spmd, %region_2.3_spmd} | conditional | flops 268893696 | bytes 31679430 | solution.py:79
  502.8 318.5 %reduce-scatter.4.cloned.1.call-done = bf16[128,4]{1,0:T(8,128)(2,1)} async-done(((bf16[4096,4]{1,0:T(8,128)(2,1)}), bf16[128,4]{1,0:T(8,128)(2,1)}) %reduce-scatter.4.cloned.1.call-update) | async-done | bytes 1040
  822.1 17.6 %psum.7 = f32[4,128]{1,0:T(4,128)S(1)} all-reduce(bf16[4,128]{1,0:T(4,128)(2,1)S(1)} %copy.50), channel_id=1, replica_groups=mesh['chan'=8,'ctx'=32] {'chan'}, use_global_device_ids=true, to_apply=%region_10.11 | all-reduce | flops 512 | bytes 3072 | tf_op jit(solution)/shard_map/psum | solution.py:106
  (179 shorter events, 222.4 us)
Async XLA Ops:
  7.2 4.5 copy-start.5
  7.2 5.3 copy-start.7
  7.2 109.0 %all-gather.5.cloned.1.call-start = ((), (), s32[]{:S(2)}) async-start(), calls=%async_computation.2 | async-start | bytes 8650752 | tf_op jit(solution)/shard_map/all_gather | solution.py:99
  8.4 115.2 %copy-start.1 = (bf16[128,1024]{0,1:T(8,128)(2,1)}, bf16[128,1024]{0,1:T(8,128)(2,1)S(1)}, u32[]{:S(2)}) copy-start(bf16[128,1024]{0,1:T(8,128)(2,1)S(1)} %copy.36) | copy-start | bytes 786436
  9.6 114.0 %copy-start.3 = (bf16[128,1024]{0,1:T(8,128)(2,1)}, bf16[128,1024]{0,1:T(8,128)(2,1)S(1)}, u32[]{:S(2)}) copy-start(bf16[128,1024]{0,1:T(8,128)(2,1)S(1)} %copy.39) | copy-start | bytes 786436
  10.4 453.2 %all-gather.3.cloned.1.call-start = ((), (), s32[]{:S(2)}) async-start(), calls=%async_computation.1 | async-start | bytes 8650752 | tf_op jit(solution)/shard_map/all_gather | solution.py:83
  362.6 108.5 %copy-start.6 = (bf16[4,8192]{1,0:T(4,128)(2,1)}, bf16[4,8192]{1,0:T(4,128)(2,1)S(1)}, u32[]{:S(2)}) copy-start(bf16[4,8192]{1,0:T(4,128)(2,1)S(1)} %get-tuple-element.458) | copy-start | bytes 196612
  362.6 2.3 copy-start
  364.7 456.6 %reduce-scatter.4.cloned.1.call-start = ((), (), s32[]{:S(2)}) async-start(), calls=%async_computation.3 | async-start | bytes 1081344
  498.1 2.8 copy-start.2
  498.1 2.8 copy-start.4
Sparse Core Ops, SparseCore 0:
  11.1 105.0 all-gather.4
  364.8 98.8 all-gather.2
  501.1 320.1 reduce-scatter.3
where the time goes:
time: 849 us; the launch traced here: 847 us
  waiting for transfers between devices  481 us (57%)
  local copies, waits for them, and re-layouts  259 us (31%)
  blocking collectives  56 us (7%)
  loops' own time  17.9 us (2%)
  matrix products  15.2 us (2%)
  between operations  14 us (2%)
    unnamed x4, waiting for transfers between devices  319 us
    all_gather x1, waiting for transfers between devices, shards(): lax.all_gather(gated, 'ctx', axis=0, tiled=True)  96.9 us
    cond x37, local copies, waits for them, and re-layouts  76.6 us
    all_gather x1, waiting for transfers between devices, shards(): lax.all_gather(back, 'ctx', axis=0, tiled=True)  65.4 us
    reshape x9, local copies, waits for them, and re-layouts, toeplitz(): return flat.reshape(padded.shape[0], height, span - 1)[:, :, :breadth]  56.2 us
    another operation x18, local copies, waits for them, and re-layouts, toeplitz(): tiled = jnp.tile(flipped, (1, height + 1))  43.2 us
    all_gather x1, blocking collectives, shards(): taps = lax.all_gather(filters, 'ctx', axis=1, tiled=True)  38.3 us
    slice x9, local copies, waits for them, and re-layouts, toeplitz(): flat = tiled[:, height - 1:height - 1 + height * (span - 1)]  24.4 us
  transfers between devices with their start and end apart: 3, of which 3 were waited for; matrix products, arithmetic and copies ran while one was open for 1% of the time, Pallas kernels for 0%

commit v1 on v0

--- a/solution.py
+++ b/solution.py
@@ -5,6 +5,11 @@
 
 D = 8192
 NFILT = 4
+
+
+def exchange_gather(array, mesh_axis, dim):
+    stack = jnp.stack([array] * lax.axis_size(mesh_axis))
+    return jnp.concatenate(lax.all_to_all(stack, mesh_axis, 0, 0), axis=dim)
 
 
 def toeplitz(padded, base, height, breadth):
@@ -80,7 +85,7 @@
 
     empty = jnp.zeros((rows, narrow, nfil), jnp.float32)
     mixed_acc, lag_part = in_blocks(
-        forward_block, (empty, lag_start), lax.all_gather(gated, "ctx", axis=0, tiled=True), rows
+        forward_block, (empty, lag_start), exchange_gather(gated, "ctx", 0), rows
     )
 
     def backward_block(grad_acc, piece, start):

time: 849 us -> 943 us (1.11)
  waiting for transfers between devices: 481 us -> 564 us
    all_to_all x0 -> x1, waiting for transfers between devices: none -> 178 us  [exchange_gather(): return jnp.concatenate(lax.all_to_all(stack, mesh_axis, 0, 0), axis=dim)]
    all_gather x1 -> x0, waiting for transfers between devices: 96.9 us -> none  [shards(): lax.all_gather(gated, 'ctx', axis=0, tiled=True)]
    while x3 -> x4, local copies, waits for them, and re-layouts: 1.72 us -> 13.2 us  [in_blocks(): result, unused = lax.scan(visit, carry, (parts, offsets))]
    unnamed x4 -> x3, waiting for transfers between devices: 319 us -> 320 us
where the time goes in v1:
time: 943 us; the launch traced here: 941 us
  waiting for transfers between devices  564 us (60%)
  local copies, waits for them, and re-layouts  267 us (28%)
  blocking collectives  56 us (6%)
  loops' own time  16.2 us (2%)
  matrix products  15.2 us (2%)
  between operations  14.3 us (2%)
    unnamed x3, waiting for transfers between devices  320 us
    all_to_all x1, waiting for transfers between devices, exchange_gather(): return jnp.concatenate(lax.all_to_all(stack, mesh_axis, 0, 0), axis=dim)  178 us
    cond x37, local copies, waits for them, and re-layouts  76.5 us
    all_gather x1, waiting for transfers between devices, shards(): lax.all_gather(back, 'ctx', axis=0, tiled=True)  65.4 us
    reshape x9, local copies, waits for them, and re-layouts, toeplitz(): return flat.reshape(padded.shape[0], height, span - 1)[:, :, :breadth]  56.2 us
    another operation x18, local copies, waits for them, and re-layouts, toeplitz(): tiled = jnp.tile(flipped, (1, height + 1))  43.2 us
    all_gather x1, blocking collectives, shards(): taps = lax.all_gather(filters, 'ctx', axis=1, tiled=True)  38.4 us
    slice x9, local copies, waits for them, and re-layouts, toeplitz(): flat = tiled[:, height - 1:height - 1 + height * (span - 1)]  24.5 us
  transfers between devices with their start and end apart: 3, of which 3 were waited for; matrix products, arithmetic and copies ran while one was open for 1% of the time, Pallas kernels for 0%

profile of v1, /device:TPU:1, one launch (start us, length us, event | category | flops | bytes accessed | tf_op | source)
XLA Modules:
  0.0 940.5 jit_solution(18432276304883272966)
XLA Ops:
  12.4 38.4 %all_gather.6 = bf16[4,4096]{1,0:T(4,128)(2,1)S(1)} all-gather(bf16[4,128]{1,0:T(4,128)(2,1)S(1)} %copy-done.7), channel_id=1, replica_groups=mesh['chan'=8,'ctx'=32] {'ctx'}, dimensions={1}, use_global_device_ids=true | all-gather | bytes 33792 | tf_op jit(solution)/shard_map/all_gather | solution.py:61
  50.8 65.4 %all-gather.2.cloned.1.call-done = bf16[4096,1024]{0,1:T(8,128)(2,1)} async-done(((bf16[128,1024]{0,1:T(8,128)(2,1)}), bf16[4096,1024]{0,1:T(8,128)(2,1)}) %all-gather.2.cloned.1.call-update) | async-done | bytes 8388624 | tf_op jit(solution)/shard_map/all_gather | solution.py:104
  116.2 7.4 copy.78
  123.7 237.5 %while.27 = (s32[]{:T(128)}, f32[128,256,4]{1,0,2:T(8,128)S(1)}, s32[8]{0:T(128)S(1)}, s32[]{:T(128)}, bf16[4,8192]{1,0:T(4,128)(2,1)S(1)}, /*index=5*/bf16[8,512,1024]{1,2,0:T(8,128)(2,1)}, s32[]{:T(128)}, s32[]{:T(128)}) while((s32[]{:T(128)}, f32[128,256,4]{1,0,2:T(8,128)S(1)}, s32[8]{0:T(128)S(1)}, s32[]{:T(128)}, ...), condition=%wide.region_8.9_spmd, body=%wide.region_5.8_spmd.sunk | while | flops 134348800 | bytes 35643552 | solution.py:51
  124.9 28.4 %conditional.5 = (f32[128,256,4]{1,0,2:T(8,128)S(1)}) conditional(s32[]{:T(128)} %convert_element_type.91, f32[128,256,4]{1,0,2:T(8,128)S(1)} %get-tuple-element.419, (s32[]{:T(128)}, s32[]{:T(128)}, bf16[4,8192]{1,0:T(4,128)(2,1)S(1)}, bf16[8,512,1024]{1,2,0:T(8,128)(2,1)}, s32[]{:T(128)}, /*index=5*/f32[128,256,4]{1,0,2:T(8,128)S(1)}) %tuple.76), branch_computations={%region_6.6_spmd, %region_7.7_spmd} | conditional | flops 134348800 | bytes 35643384 | solution.py:101
  143.3 6.8 reshape.54
  154.6 28.4 %conditional.5 = (f32[128,256,4]{1,0,2:T(8,128)S(1)}) conditional(s32[]{:T(128)} %convert_element_type.91, f32[128,256,4]{1,0,2:T(8,128)S(1)} %get-tuple-element.419, (s32[]{:T(128)}, s32[]{:T(128)}, bf16[4,8192]{1,0:T(4,128)(2,1)S(1)}, bf16[8,512,1024]{1,2,0:T(8,128)(2,1)}, s32[]{:T(128)}, /*index=5*/f32[128,256,4]{1,0,2:T(8,128)S(1)}) %tuple.76), branch_computations={%region_6.6_spmd, %region_7.7_spmd} | conditional | flops 134348800 | bytes 35643384 | solution.py:101
  184.3 28.4 %conditional.5 = (f32[128,256,4]{1,0,2:T(8,128)S(1)}) conditional(s32[]{:T(128)} %convert_element_type.91, f32[128,256,4]{1,0,2:T(8,128)S(1)} %get-tuple-element.419, (s32[]{:T(128)}, s32[]{:T(128)}, bf16[4,8192]{1,0:T(4,128)(2,1)S(1)}, bf16[8,512,1024]{1,2,0:T(8,128)(2,1)}, s32[]{:T(128)}, /*index=5*/f32[128,256,4]{1,0,2:T(8,128)S(1)}) %tuple.76), branch_computations={%region_6.6_spmd, %region_7.7_spmd} | conditional | flops 134348800 | bytes 35643384 | solution.py:101
  202.6 6.8 reshape.54
  213.9 28.4 %conditional.5 = (f32[128,256,4]{1,0,2:T(8,128)S(1)}) conditional(s32[]{:T(128)} %convert_element_type.91, f32[128,256,4]{1,0,2:T(8,128)S(1)} %get-tuple-element.419, (s32[]{:T(128)}, s32[]{:T(128)}, bf16[4,8192]{1,0:T(4,128)(2,1)S(1)}, bf16[8,512,1024]{1,2,0:T(8,128)(2,1)}, s32[]{:T(128)}, /*index=5*/f32[128,256,4]{1,0,2:T(8,128)S(1)}) %tuple.76), branch_computations={%region_6.6_spmd, %region_7.7_spmd} | conditional | flops 134348800 | bytes 35643384 | solution.py:101
  232.3 6.8 reshape.54
  243.6 28.4 %conditional.5 = (f32[128,256,4]{1,0,2:T(8,128)S(1)}) conditional(s32[]{:T(128)} %convert_element_type.91, f32[128,256,4]{1,0,2:T(8,128)S(1)} %get-tuple-element.419, (s32[]{:T(128)}, s32[]{:T(128)}, bf16[4,8192]{1,0:T(4,128)(2,1)S(1)}, bf16[8,512,1024]{1,2,0:T(8,128)(2,1)}, s32[]{:T(128)}, /*index=5*/f32[128,256,4]{1,0,2:T(8,128)S(1)}) %tuple.76), branch_computations={%region_6.6_spmd, %region_7.7_spmd} | conditional | flops 134348800 | bytes 35643384 | solution.py:101
  262.0 6.8 reshape.54
  273.3 28.4 %conditional.5 = (f32[128,256,4]{1,0,2:T(8,128)S(1)}) conditional(s32[]{:T(128)} %convert_element_type.91, f32[128,256,4]{1,0,2:T(8,128)S(1)} %get-tuple-element.419, (s32[]{:T(128)}, s32[]{:T(128)}, bf16[4,8192]{1,0:T(4,128)(2,1)S(1)}, bf16[8,512,1024]{1,2,0:T(8,128)(2,1)}, s32[]{:T(128)}, /*index=5*/f32[128,256,4]{1,0,2:T(8,128)S(1)}) %tuple.76), branch_computations={%region_6.6_spmd, %region_7.7_spmd} | conditional | flops 134348800 | bytes 35643384 | solution.py:101
  291.6 6.8 reshape.54
  302.9 28.4 %conditional.5 = (f32[128,256,4]{1,0,2:T(8,128)S(1)}) conditional(s32[]{:T(128)} %convert_element_type.91, f32[128,256,4]{1,0,2:T(8,128)S(1)} %get-tuple-element.419, (s32[]{:T(128)}, s32[]{:T(128)}, bf16[4,8192]{1,0:T(4,128)(2,1)S(1)}, bf16[8,512,1024]{1,2,0:T(8,128)(2,1)}, s32[]{:T(128)}, /*index=5*/f32[128,256,4]{1,0,2:T(8,128)S(1)}) %tuple.76), branch_computations={%region_6.6_spmd, %region_7.7_spmd} | conditional | flops 134348800 | bytes 35643384 | solution.py:101
  321.3 6.8 reshape.54
  332.6 28.4 %conditional.5 = (f32[128,256,4]{1,0,2:T(8,128)S(1)}) conditional(s32[]{:T(128)} %convert_element_type.91, f32[128,256,4]{1,0,2:T(8,128)S(1)} %get-tuple-element.419, (s32[]{:T(128)}, s32[]{:T(128)}, bf16[4,8192]{1,0:T(4,128)(2,1)S(1)}, bf16[8,512,1024]{1,2,0:T(8,128)(2,1)}, s32[]{:T(128)}, /*index=5*/f32[128,256,4]{1,0,2:T(8,128)S(1)}) %tuple.76), branch_computations={%region_6.6_spmd, %region_7.7_spmd} | conditional | flops 134348800 | bytes 35643384 | solution.py:101
  374.1 178.1 %all-to-all-done = bf16[32,128,1024]{2,1,0:T(8,128)(2,1)} async-done(((bf16[32,128,1024]{2,1,0:T(8,128)(2,1)}), bf16[32,128,1024]{2,1,0:T(8,128)(2,1)}, u32[]{:S(2)}, u32[]{:S(2)}) %all-to-all-start) | async-done | bytes 8388640 | tf_op jit(solution)/shard_map/all_to_all | solution.py:12
  552.2 11.5 %copy.60 = bf16[8,512,1024]{1,2,0:T(8,128)(2,1)} copy(bf16[8,512,1024]{2,1,0:T(8,128)(2,1)} %bitcast.5) | data formatting | bytes 16777216 | tf_op jit(solution)/shard_map/while | solution.py:51
  564.5 25.1 %while.26 = (s32[]{:T(128)}, f32[128,256,4]{1,0,2:T(8,128)}, f32[4,8192]{1,0:T(4,128)S(1)}, s32[8]{0:T(128)S(1)}, s32[]{:T(128)}, /*index=5*/s32[]{:T(128)}, bf1...) while((s32[]{:T(128)}, f32[128,256,4]{1,0,2:T(8,128)}, ...), condition=%wide.region_4.5_spmd, body=%wide.region_0.4_spmd.sunk | while | flops 268893696 | bytes 31679636 | solution.py:51
  565.6 15.9 %conditional.4 = ((f32[128,256,4]{1,0,2:T(8,128)}, f32[4,8192]{1,0:T(4,128)S(1)})) conditional(s32[]{:T(128)} %convert_element_type.90, (f32[128,256,4]{1,0,2:T(8,128)}, f32[4,8192]{1,0:T(4,128)S(1)}) %tuple.73, (s32[]{:T(128)}, s32[]{:T(128)}, bf16[4,8192]{1,0:T(4,128)(2,1)}, bf16[8,512,1024]{1,2,0:T(8,128)(2,1)}, s32[]{:T(128)}, ...), branch_computations={%region_1.1_spmd, %region_2.3_spmd} | conditional | flops 268893696 | bytes 31679430 | solution.py:84
  594.2 320.4 %reduce-scatter.4.cloned.1.call-done = bf16[128,4]{1,0:T(8,128)(2,1)} async-done(((bf16[4096,4]{1,0:T(8,128)(2,1)}), bf16[128,4]{1,0:T(8,128)(2,1)}) %reduce-scatter.4.cloned.1.call-update) | async-done | bytes 1040
  915.4 17.7 %psum.7 = f32[4,128]{1,0:T(4,128)S(1)} all-reduce(bf16[4,128]{1,0:T(4,128)(2,1)S(1)} %copy.70), channel_id=1, replica_groups=mesh['chan'=8,'ctx'=32] {'chan'}, use_global_device_ids=true, to_apply=%region_10.11 | all-reduce | flops 512 | bytes 3072 | tf_op jit(solution)/shard_map/psum | solution.py:111
  (180 shorter events, 230.3 us)
Async XLA Ops:
  7.2 4.4 copy-start.5
  7.2 5.2 copy-start.7
  7.2 109.0 %all-gather.2.cloned.1.call-start = ((), (), s32[]{:S(2)}) async-start(), calls=%async_computation.2 | async-start | bytes 8650752 | tf_op jit(solution)/shard_map/all_gather | solution.py:104
  8.4 115.2 %copy-start.1 = (bf16[128,1024]{0,1:T(8,128)(2,1)}, bf16[128,1024]{0,1:T(8,128)(2,1)S(1)}, u32[]{:S(2)}) copy-start(bf16[128,1024]{0,1:T(8,128)(2,1)S(1)} %copy.55) | copy-start | bytes 786436
  9.6 114.0 %copy-start.3 = (bf16[128,1024]{0,1:T(8,128)(2,1)}, bf16[128,1024]{0,1:T(8,128)(2,1)S(1)}, u32[]{:S(2)}) copy-start(bf16[128,1024]{0,1:T(8,128)(2,1)S(1)} %copy.59) | copy-start | bytes 786436
  361.2 5.8 copy-start.6
  367.0 5.2 copy-start
  367.0 185.2 %all-to-all-start = ((bf16[32,128,1024]{2,1,0:T(8,128)(2,1)}), bf16[32,128,1024]{2,1,0:T(8,128)(2,1)}, u32[]{:S(2)}, u32[]{:S(2)}) async-start(bf16[32,128,1024]{2,1,0:T(8,128)(2,1)} %stack.2), calls=%async_computation | async-start | bytes 16777216 | tf_op jit(solution)/shard_map/all_to_all | solution.py:12
  372.1 542.5 %reduce-scatter.4.cloned.1.call-start = ((), (), s32[]{:S(2)}) async-start(), calls=%async_computation.3 | async-start | bytes 1081344
  589.6 2.8 copy-start.2
  589.6 2.8 copy-start.4
Sparse Core Ops, SparseCore 0:
  11.1 105.1 all-gather.1
  592.5 322.0 reduce-scatter.3
